TPU v7x, 32 devices: a whole 2x2x4 slice. The times are simulated.
32 devices in a mesh: row: 8 (over y, x, core), rep: 4 (over z).
Axes of the slice: x: 2, y: 2, z: 4, core: 2. Of those that a mesh axis runs over, the one named last changes fastest.
Arguments:
- features: float32 [16384, 256], P('row'), may hold values from -6 to 6
- adjacency_tiles: float32 [8, 4, 256, 128, 128], P('row', 'rep'), may hold values from -0.25 to 0.25
- tile_rows: int32 [8, 4, 256], P('row', 'rep'), may hold values from 0 to 15, as said below
- tile_cols: int32 [8, 4, 256], P('row', 'rep'), may hold values from 0 to 31, as said below
- tile_counts: int32 [8, 4], P('row', 'rep'), may hold values from 32 to 256, as said below
- plan: int32 [4, 2], replicated, may hold values from 0 to 7, as said below
- weights: float32 [2, 256, 256], replicated, may hold values from -0.375 to 0.375
Outputs:
- embedded: float32 [16384, 256], P(('row', 'rep'))
Inputs may be any that keep to these rules, and one draw needn't show every extreme that they name: Within one block row and replica the listed positions (tile_rows, tile_cols) are distinct. Within one block row and replica the listed positions (tile_rows, tile_cols) are distinct. `tile_counts`: some block row and replica lists exactly 256 tiles. `plan`: every block row 0 to 7 appears exactly once in the table.
All inputs are finite; a program needn't handle non-finite values.
Results may differ from a plain program's by a relative error of at most 0.0003.
Values sent between devices are 32-bit elements; how exact they have to be, the bound alone decides.
No kernel may reach another device: no remote copies, remote signals or barrier semaphores. Data moves between devices by JAX's collectives and lax.ppermute only.
A program may use at most 128 MiB of HBM per device.

v0:
```python
import math
import jax
import jax.numpy as jnp
from jax import lax
from jax.sharding import PartitionSpec as P


def from_root(value, axis, source):
    kept = jnp.where(lax.axis_index(axis) == source, value, 0).astype(value.dtype)
    return lax.psum(kept, axis)


def tile_sum(received, tiles_here, rows_here, cols_here, count_here, row_tiles):
    tile_slots = tiles_here.shape[0]
    tile_edge = received.shape[1]
    feat_width = received.shape[2]
    group_size = math.gcd(tile_slots, 64)
    steps_total = tile_slots // group_size
    slot_ids = jnp.arange(tile_slots, dtype=jnp.int32)
    live_mask = (slot_ids < count_here).astype(jnp.float32)
    lane_ids = jnp.arange(row_tiles, dtype=jnp.int32)

    def advance(running, packet):
        block_tiles, block_rows, block_cols, block_live = packet
        sources = jnp.take(received, block_cols, axis=0)
        product = jnp.einsum("tij,tjf->tif", block_tiles, sources, precision=lax.Precision.HIGHEST)
        product = product * block_live[:, None, None]
        placing = (block_rows[None, :] == lane_ids[:, None]).astype(jnp.float32)
        added = jnp.dot(
            placing,
            product.reshape(group_size, tile_edge * feat_width),
            precision=lax.Precision.HIGHEST,
        )
        return (running + added, None)

    packets = (
        tiles_here.reshape(steps_total, group_size, tile_edge, tile_edge),
        rows_here.reshape(steps_total, group_size),
        cols_here.reshape(steps_total, group_size),
        live_mask.reshape(steps_total, group_size),
    )
    start = jnp.zeros((row_tiles, tile_edge * feat_width), jnp.float32)
    running, unused = lax.scan(advance, start, packets)
    return running.reshape(row_tiles * tile_edge, feat_width)


def shards(features, adjacency_tiles, tile_rows, tile_cols, tile_counts, plan, weights):
    replica = lax.axis_index("rep")
    block_len = features.shape[0]
    feat_width = features.shape[1]
    tile_edge = adjacency_tiles.shape[-1]
    row_tiles = block_len // tile_edge
    section_total = plan.shape[1]
    layer_total = weights.shape[0]
    section_roots = lax.dynamic_index_in_dim(plan, replica, 0, keepdims=False)
    tiles_here = adjacency_tiles[0, 0]
    rows_here = tile_rows[0, 0]
    cols_here = tile_cols[0, 0]
    count_here = tile_counts[0, 0]
    current = features
    result = features
    for layer_num in range(layer_total):
        received = jnp.zeros((section_total * block_len, feat_width), jnp.float32)
        for section_num in range(section_total):
            root_now = lax.dynamic_index_in_dim(section_roots, section_num, 0, keepdims=False)
            arrived = from_root(current, "row", root_now)
            received = lax.dynamic_update_slice_in_dim(
                received, arrived, section_num * block_len, 0
            )
        received = received.reshape(section_total * row_tiles, tile_edge, feat_width)
        partial_value = tile_sum(received, tiles_here, rows_here, cols_here, count_here, row_tiles)
        my_share = lax.psum_scatter(partial_value, "rep", scatter_dimension=0, tiled=True)
        result = jnp.maximum(
            jnp.dot(my_share, weights[layer_num], precision=lax.Precision.HIGHEST), 0.0
        )
        if layer_num + 1 < layer_total:
            current = lax.all_gather(result, "rep", axis=0, tiled=True)
    return result


def solution(mesh):
    return jax.shard_map(
        shards,
        mesh=mesh,
        in_specs=(
            P("row", None),
            P("row", "rep", None, None, None),
            P("row", "rep", None),
            P("row", "rep", None),
            P("row", "rep"),
            P(),
            P(),
        ),
        out_specs=P(("row", "rep"), None),
        check_vma=False,
    )
```

profile of v0, /device:TPU:0, one launch (start us, length us, event | category | flops | bytes accessed | tf_op | source)
XLA Modules:
  0.0 589.2 jit_solution(12762534406502106215)
XLA Ops:
  15.7 81.0 %all-reduce.7.cloned.1.call-done = (f32[2048,256]{1,0:T(8,128)}, f32[2048,256]{1,0:T(8,128)}) async-done(((f32[2048,256]{1,0:T(8,128)}, f32[2048,256]{1,0:T(8,128)}), (f32[2048,256]{1,0:T(8,128)}, f32[2048,256]{1,0:T(8,128)})) %all-reduce.7.cloned.1.call-update) | async-done | bytes 4194320 | tf_op jit(solution)/shard_map/psum | solution.py:10
  101.1 126.4 %while.22 = (s32[]{:T(128)}, f32[16,32768]{1,0:T(8,128)S(1)}, s32[4,64]{1,0:T(4,128)S(1)}, f32[4,64,128,128]{3,2,1,0:T(8,128)}, s32[4,64]{1,0:T(4,128)S(1)}, /*i...) while((s32[]{:T(128)}, f32[16,32768]{1,0:T(8,128)S(1)}, ...), condition=%wide.region_3.5_spmd.clone, body=%wide.region_2.4_spmd.clone.sunk | while | flops 3629124096 | bytes 67116272 | solution.py:43
  101.1 6.5 %gather_fusion = f32[64,128,256]{2,1,0:T(8,128)} fusion(f32[32,128,256]{2,1,0:T(8,128)} %get-tuple-element.303, s32[1024]{0:T(1024)S(1)} %pad_clamp_fusion.4), kind=kCustom, calls=%fused_computation.clone.clone.1 | custom fusion | bytes 16777472 | tf_op jit(solution)/shard_map/while/body/eval_jaxpr/jit(_take)/gather | solution.py:25
  107.6 11.7 %broadcast_multiply_fusion.4 = f32[64,128,256]{2,1,0:T(8,128)S(1)} fusion(f32[64]{0:T(128)S(1)} %fusion.59, f32[64,128,256]{2,1,0:T(8,128)} %gather_fusion, pred[64]{0:T(512)(128)(4,1)S(1)} %get-tuple-element.270, f32[4,64,128,128]{3,2,1,0:T(8,128)} %get-tuple-element.301, s32[]{:T(128)} %get-tuple-element.289), kind=kOutput, calls=%fused_computation.9.clone.1 | convolution fusion | flops 3225419776 | bytes 20972352 | tf_op jit(solution)/shard_map/while/body/eval_jaxpr/tij,tjf->tif/dot_general | solution.py:26
  119.4 8.0 %copy.12 = f32[8,8,128,256]{3,1,2,0:T(8,128)} copy(f32[8,8,128,256]{3,2,1,0:T(8,128)S(1)} %bitcast.75) | data formatting | bytes 16777216 | tf_op jit(solution)/shard_map/while
  127.3 5.3 convolution_add_fusion.4
  132.7 6.5 %gather_fusion = f32[64,128,256]{2,1,0:T(8,128)} fusion(f32[32,128,256]{2,1,0:T(8,128)} %get-tuple-element.303, s32[1024]{0:T(1024)S(1)} %pad_clamp_fusion.4), kind=kCustom, calls=%fused_computation.clone.clone.1 | custom fusion | bytes 16777472 | tf_op jit(solution)/shard_map/while/body/eval_jaxpr/jit(_take)/gather | solution.py:25
  139.2 11.7 %broadcast_multiply_fusion.4 = f32[64,128,256]{2,1,0:T(8,128)S(1)} fusion(f32[64]{0:T(128)S(1)} %fusion.59, f32[64,128,256]{2,1,0:T(8,128)} %gather_fusion, pred[64]{0:T(512)(128)(4,1)S(1)} %get-tuple-element.270, f32[4,64,128,128]{3,2,1,0:T(8,128)} %get-tuple-element.301, s32[]{:T(128)} %get-tuple-element.289), kind=kOutput, calls=%fused_computation.9.clone.1 | convolution fusion | flops 3225419776 | bytes 20972352 | tf_op jit(solution)/shard_map/while/body/eval_jaxpr/tij,tjf->tif/dot_general | solution.py:26
  151.0 8.0 %copy.12 = f32[8,8,128,256]{3,1,2,0:T(8,128)} copy(f32[8,8,128,256]{3,2,1,0:T(8,128)S(1)} %bitcast.75) | data formatting | bytes 16777216 | tf_op jit(solution)/shard_map/while
  164.3 6.5 %gather_fusion = f32[64,128,256]{2,1,0:T(8,128)} fusion(f32[32,128,256]{2,1,0:T(8,128)} %get-tuple-element.303, s32[1024]{0:T(1024)S(1)} %pad_clamp_fusion.4), kind=kCustom, calls=%fused_computation.clone.clone.1 | custom fusion | bytes 16777472 | tf_op jit(solution)/shard_map/while/body/eval_jaxpr/jit(_take)/gather | solution.py:25
  170.8 11.7 %broadcast_multiply_fusion.4 = f32[64,128,256]{2,1,0:T(8,128)S(1)} fusion(f32[64]{0:T(128)S(1)} %fusion.59, f32[64,128,256]{2,1,0:T(8,128)} %gather_fusion, pred[64]{0:T(512)(128)(4,1)S(1)} %get-tuple-element.270, f32[4,64,128,128]{3,2,1,0:T(8,128)} %get-tuple-element.301, s32[]{:T(128)} %get-tuple-element.289), kind=kOutput, calls=%fused_computation.9.clone.1 | convolution fusion | flops 3225419776 | bytes 20972352 | tf_op jit(solution)/shard_map/while/body/eval_jaxpr/tij,tjf->tif/dot_general | solution.py:26
  182.6 8.0 %copy.12 = f32[8,8,128,256]{3,1,2,0:T(8,128)} copy(f32[8,8,128,256]{3,2,1,0:T(8,128)S(1)} %bitcast.75) | data formatting | bytes 16777216 | tf_op jit(solution)/shard_map/while
  196.0 6.5 %gather_fusion = f32[64,128,256]{2,1,0:T(8,128)} fusion(f32[32,128,256]{2,1,0:T(8,128)} %get-tuple-element.303, s32[1024]{0:T(1024)S(1)} %pad_clamp_fusion.4), kind=kCustom, calls=%fused_computation.clone.clone.1 | custom fusion | bytes 16777472 | tf_op jit(solution)/shard_map/while/body/eval_jaxpr/jit(_take)/gather | solution.py:25
  202.5 11.7 %broadcast_multiply_fusion.4 = f32[64,128,256]{2,1,0:T(8,128)S(1)} fusion(f32[64]{0:T(128)S(1)} %fusion.59, f32[64,128,256]{2,1,0:T(8,128)} %gather_fusion, pred[64]{0:T(512)(128)(4,1)S(1)} %get-tuple-element.270, f32[4,64,128,128]{3,2,1,0:T(8,128)} %get-tuple-element.301, s32[]{:T(128)} %get-tuple-element.289), kind=kOutput, calls=%fused_computation.9.clone.1 | convolution fusion | flops 3225419776 | bytes 20972352 | tf_op jit(solution)/shard_map/while/body/eval_jaxpr/tij,tjf->tif/dot_general | solution.py:26
  214.2 8.0 %copy.12 = f32[8,8,128,256]{3,1,2,0:T(8,128)} copy(f32[8,8,128,256]{3,2,1,0:T(8,128)S(1)} %bitcast.75) | data formatting | bytes 16777216 | tf_op jit(solution)/shard_map/while
  229.3 43.6 %reduce-scatter.3.cloned.1.call-done = f32[512,256]{1,0:T(8,128)} async-done(((f32[2048,256]{1,0:T(8,128)}), f32[512,256]{1,0:T(8,128)}) %reduce-scatter.3.cloned.1.call-update) | async-done | bytes 524304 | tf_op jit(solution)/shard_map/reduce_scatter | solution.py:72
  275.4 45.0 %all-gather.2.cloned.1.call-done = f32[2048,256]{1,0:T(8,128)} async-done(((f32[512,256]{1,0:T(8,128)}), f32[2048,256]{1,0:T(8,128)}) %all-gather.2.cloned.1.call-update) | async-done | bytes 2097168 | tf_op jit(solution)/shard_map/all_gather | solution.py:77
  324.3 79.7 %all-reduce.5.cloned.1.call-done = (f32[2048,256]{1,0:T(8,128)}, f32[2048,256]{1,0:T(8,128)}) async-done(((f32[2048,256]{1,0:T(8,128)}, f32[2048,256]{1,0:T(8,128)}), (f32[2048,256]{1,0:T(8,128)}, f32[2048,256]{1,0:T(8,128)})) %all-reduce.5.cloned.1.call-update) | async-done | bytes 4194320 | tf_op jit(solution)/shard_map/psum | solution.py:10
  408.5 126.4 %while.23 = (s32[]{:T(128)}, f32[16,32768]{1,0:T(8,128)S(1)}, s32[4,64]{1,0:T(4,128)S(1)}, f32[4,64,128,128]{3,2,1,0:T(8,128)}, s32[4,64]{1,0:T(4,128)S(1)}, /*i...) while((s32[]{:T(128)}, f32[16,32768]{1,0:T(8,128)S(1)}, ...), condition=%wide.region_8.10_spmd.clone, body=%wide.region_7.9_spmd.clone.sunk | while | flops 3629124096 | bytes 67116272 | solution.py:43
  408.5 6.5 %gather_fusion.1 = f32[64,128,256]{2,1,0:T(8,128)} fusion(f32[32,128,256]{2,1,0:T(8,128)} %get-tuple-element.330, s32[1024]{0:T(1024)S(1)} %pad_clamp_fusion.5), kind=kCustom, calls=%fused_computation.1.clone.clone.1 | custom fusion | bytes 16777472 | tf_op jit(solution)/shard_map/while/body/eval_jaxpr/jit(_take)/gather | solution.py:25
  415.0 11.7 %broadcast_multiply_fusion.5 = f32[64,128,256]{2,1,0:T(8,128)S(1)} fusion(f32[64]{0:T(128)S(1)} %fusion.64, f32[64,128,256]{2,1,0:T(8,128)} %gather_fusion.1, pred[64]{0:T(512)(128)(4,1)S(1)} %get-tuple-element.279, f32[4,64,128,128]{3,2,1,0:T(8,128)} %get-tuple-element.328, s32[]{:T(128)} %get-tuple-element.316), kind=kOutput, calls=%fused_computation.30.clone.1 | convolution fusion | flops 3225419776 | bytes 20972352 | tf_op jit(solution)/shard_map/while/body/eval_jaxpr/tij,tjf->tif/dot_general | solution.py:26
  426.8 8.0 %copy.13 = f32[8,8,128,256]{3,1,2,0:T(8,128)} copy(f32[8,8,128,256]{3,2,1,0:T(8,128)S(1)} %bitcast.76) | data formatting | bytes 16777216 | tf_op jit(solution)/shard_map/while
  440.1 6.5 %gather_fusion.1 = f32[64,128,256]{2,1,0:T(8,128)} fusion(f32[32,128,256]{2,1,0:T(8,128)} %get-tuple-element.330, s32[1024]{0:T(1024)S(1)} %pad_clamp_fusion.5), kind=kCustom, calls=%fused_computation.1.clone.clone.1 | custom fusion | bytes 16777472 | tf_op jit(solution)/shard_map/while/body/eval_jaxpr/jit(_take)/gather | solution.py:25
  446.6 11.7 %broadcast_multiply_fusion.5 = f32[64,128,256]{2,1,0:T(8,128)S(1)} fusion(f32[64]{0:T(128)S(1)} %fusion.64, f32[64,128,256]{2,1,0:T(8,128)} %gather_fusion.1, pred[64]{0:T(512)(128)(4,1)S(1)} %get-tuple-element.279, f32[4,64,128,128]{3,2,1,0:T(8,128)} %get-tuple-element.328, s32[]{:T(128)} %get-tuple-element.316), kind=kOutput, calls=%fused_computation.30.clone.1 | convolution fusion | flops 3225419776 | bytes 20972352 | tf_op jit(solution)/shard_map/while/body/eval_jaxpr/tij,tjf->tif/dot_general | solution.py:26
  458.4 8.0 %copy.13 = f32[8,8,128,256]{3,1,2,0:T(8,128)} copy(f32[8,8,128,256]{3,2,1,0:T(8,128)S(1)} %bitcast.76) | data formatting | bytes 16777216 | tf_op jit(solution)/shard_map/while
  471.7 6.5 %gather_fusion.1 = f32[64,128,256]{2,1,0:T(8,128)} fusion(f32[32,128,256]{2,1,0:T(8,128)} %get-tuple-element.330, s32[1024]{0:T(1024)S(1)} %pad_clamp_fusion.5), kind=kCustom, calls=%fused_computation.1.clone.clone.1 | custom fusion | bytes 16777472 | tf_op jit(solution)/shard_map/while/body/eval_jaxpr/jit(_take)/gather | solution.py:25
  478.2 11.7 %broadcast_multiply_fusion.5 = f32[64,128,256]{2,1,0:T(8,128)S(1)} fusion(f32[64]{0:T(128)S(1)} %fusion.64, f32[64,128,256]{2,1,0:T(8,128)} %gather_fusion.1, pred[64]{0:T(512)(128)(4,1)S(1)} %get-tuple-element.279, f32[4,64,128,128]{3,2,1,0:T(8,128)} %get-tuple-element.328, s32[]{:T(128)} %get-tuple-element.316), kind=kOutput, calls=%fused_computation.30.clone.1 | convolution fusion | flops 3225419776 | bytes 20972352 | tf_op jit(solution)/shard_map/while/body/eval_jaxpr/tij,tjf->tif/dot_general | solution.py:26
  490.0 8.0 %copy.13 = f32[8,8,128,256]{3,1,2,0:T(8,128)} copy(f32[8,8,128,256]{3,2,1,0:T(8,128)S(1)} %bitcast.76) | data formatting | bytes 16777216 | tf_op jit(solution)/shard_map/while
  503.3 6.5 %gather_fusion.1 = f32[64,128,256]{2,1,0:T(8,128)} fusion(f32[32,128,256]{2,1,0:T(8,128)} %get-tuple-element.330, s32[1024]{0:T(1024)S(1)} %pad_clamp_fusion.5), kind=kCustom, calls=%fused_computation.1.clone.clone.1 | custom fusion | bytes 16777472 | tf_op jit(solution)/shard_map/while/body/eval_jaxpr/jit(_take)/gather | solution.py:25
  509.8 11.7 %broadcast_multiply_fusion.5 = f32[64,128,256]{2,1,0:T(8,128)S(1)} fusion(f32[64]{0:T(128)S(1)} %fusion.64, f32[64,128,256]{2,1,0:T(8,128)} %gather_fusion.1, pred[64]{0:T(512)(128)(4,1)S(1)} %get-tuple-element.279, f32[4,64,128,128]{3,2,1,0:T(8,128)} %get-tuple-element.328, s32[]{:T(128)} %get-tuple-element.316), kind=kOutput, calls=%fused_computation.30.clone.1 | convolution fusion | flops 3225419776 | bytes 20972352 | tf_op jit(solution)/shard_map/while/body/eval_jaxpr/tij,tjf->tif/dot_general | solution.py:26
  521.6 8.0 %copy.13 = f32[8,8,128,256]{3,1,2,0:T(8,128)} copy(f32[8,8,128,256]{3,2,1,0:T(8,128)S(1)} %bitcast.76) | data formatting | bytes 16777216 | tf_op jit(solution)/shard_map/while
  536.4 43.8 %reduce-scatter.5.cloned.1.call-done = f32[512,256]{1,0:T(8,128)} async-done(((f32[2048,256]{1,0:T(8,128)}), f32[512,256]{1,0:T(8,128)}) %reduce-scatter.5.cloned.1.call-update) | async-done | bytes 524304 | tf_op jit(solution)/shard_map/reduce_scatter | solution.py:72
  (77 shorter events, 65.8 us)
Async XLA Ops:
  6.5 0.7 copy-start
  6.5 90.1 %all-reduce.7.cloned.1.call-start = ((), (), s32[]{:S(2)}) async-start(), calls=%async_computation.6 | async-start | bytes 8388608 | tf_op jit(solution)/shard_map/psum | solution.py:10
  9.0 4.5 copy-start.3
  9.0 5.2 copy-start.4
  12.9 260.0 %reduce-scatter.3.cloned.1.call-start = ((), (), s32[]{:S(2)}) async-start(), calls=%async_computation.2 | async-start | bytes 2621440 | tf_op jit(solution)/shard_map/reduce_scatter | solution.py:72
  227.5 45.4 %copy-start.2 = (f32[2,256,256]{2,1,0:T(8,128)S(1)}, f32[2,256,256]{2,1,0:T(8,128)}, u32[]{:S(2)}) copy-start(f32[2,256,256]{2,1,0:T(8,128)} %param.19) | copy-start | bytes 1572868
  229.1 91.3 %all-gather.2.cloned.1.call-start = ((), (), s32[]{:S(2)}) async-start(), calls=%async_computation.3 | async-start | bytes 2621440 | tf_op jit(solution)/shard_map/all_gather | solution.py:77
  275.4 128.7 %all-reduce.5.cloned.1.call-start = ((), (), s32[]{:S(2)}) async-start(), calls=%async_computation.5 | async-start | bytes 8388608 | tf_op jit(solution)/shard_map/psum | solution.py:10
  324.2 256.1 %reduce-scatter.5.cloned.1.call-start = ((), (), s32[]{:S(2)}) async-start(), calls=%async_computation.4 | async-start | bytes 2621440 | tf_op jit(solution)/shard_map/reduce_scatter | solution.py:72
  534.9 47.8 %copy-start.1 = (s32[4,2]{0,1:T(2,128)S(1)}, s32[4,2]{0,1:T(2,128)}, u32[]{:S(2)}) copy-start(s32[4,2]{0,1:T(2,128)} %param.18) | copy-start | bytes 100
Sparse Core Ops, SparseCore 0:
  13.0 83.5 all-reduce.6
  229.2 43.6 reduce-scatter.2
  275.5 44.8 all-gather.1
  324.4 79.6 all-reduce.4
  536.6 43.6 reduce-scatter.4
where the time goes:
time: 590 us; the launch traced here: 589 us
  waiting for transfers between devices  293 us (50%)
  matrix products  141 us (24%)
  local copies, waits for them, and re-layouts  121 us (21%)
  other arithmetic  18.1 us (3%)
  between operations  15.1 us (3%)
    psum x2, waiting for transfers between devices, from_root(): return lax.psum(kept, axis)  161 us
    dot_general x8, matrix products, advance(): jnp.einsum('tij,tjf->tif', block_tiles, sources, precision=lax.Precision....  93.9 us
    reduce_scatter x2, waiting for transfers between devices, shards(): lax.psum_scatter(partial_value, 'rep', scatter_dimension=0, tiled=True)  87.5 us
    while x8, local copies, waits for them, and re-layouts  63.7 us
    gather x8, local copies, waits for them, and re-layouts, advance(): sources = jnp.take(received, block_cols, axis=0)  52 us
    all_gather x1, waiting for transfers between devices, shards(): current = lax.all_gather(result, 'rep', axis=0, tiled=True)  45 us
    dot_general x8, matrix products, advance(): jnp.dot(placing, product.reshape(group_size, tile_edge * feat_width), pre...  42.7 us
  transfers between devices with their start and end apart: 5, of which 5 were waited for; matrix products, arithmetic and copies ran while one was open for 0% of the time, Pallas kernels for 0%

commit v1 on v0

--- a/solution.py
+++ b/solution.py
@@ -5,9 +5,15 @@
 from jax.sharding import PartitionSpec as P
 
 
+def summed_here(x, axis):
+    blocks = lax.all_gather(x, axis, axis=0, tiled=False)
+    total = blocks.sum(axis=0)
+    return total
+
+
 def from_root(value, axis, source):
     kept = jnp.where(lax.axis_index(axis) == source, value, 0).astype(value.dtype)
-    return lax.psum(kept, axis)
+    return summed_here(kept, axis)
 
 
 def tile_sum(received, tiles_here, rows_here, cols_here, count_here, row_tiles):

time: 590 us -> 808 us (1.37)
  waiting for transfers between devices: 293 us -> 477 us
  other arithmetic: 18.1 us -> 52.2 us
    all_gather x0 -> x4, waiting for transfers between devices: none -> 343 us  [summed_here(): blocks = lax.all_gather(x, axis, axis=0, tiled=False)]
    psum x2 -> x0, waiting for transfers between devices: 161 us -> none  [from_root(): return lax.psum(kept, axis)]
    reduce_sum x0 -> x4, other arithmetic: none -> 34 us  [summed_here(): total = blocks.sum(axis=0)]
  transfers between devices with their start and end apart: 5 -> 7, of which waited for: 5 -> 7; matrix products, arithmetic and copies ran while one was open for 0% -> 2% of each run, Pallas kernels for 0% -> 0%
where the time goes in v1:
time: 808 us
  waiting for transfers between devices  477 us (59%)
  matrix products  141 us (17%)
  local copies, waits for them, and re-layouts  121 us (15%)
  other arithmetic  52.2 us (6%)
  between operations  15.5 us (2%)
    all_gather x4, waiting for transfers between devices, summed_here(): blocks = lax.all_gather(x, axis, axis=0, tiled=False)  343 us
    dot_general x8, matrix products, advance(): jnp.einsum('tij,tjf->tif', block_tiles, sources, precision=lax.Precision....  93.9 us
    reduce_scatter x2, waiting for transfers between devices, shards(): lax.psum_scatter(partial_value, 'rep', scatter_dimension=0, tiled=True)  87.3 us
    while x8, local copies, waits for them, and re-layouts  63.7 us
    gather x8, local copies, waits for them, and re-layouts, advance(): sources = jnp.take(received, block_cols, axis=0)  52 us
    all_gather x1, waiting for transfers between devices, shards(): current = lax.all_gather(result, 'rep', axis=0, tiled=True)  45 us
    dot_general x8, matrix products, advance(): jnp.dot(placing, product.reshape(group_size, tile_edge * feat_width), pre...  42.7 us
    reduce_sum x4, other arithmetic, summed_here(): total = blocks.sum(axis=0)  34 us
  transfers between devices with their start and end apart: 7, of which 7 were waited for; matrix products, arithmetic and copies ran while one was open for 2% of the time, Pallas kernels for 0%

profile of v1, /device:TPU:0, one launch (start us, length us, event | category | flops | bytes accessed | tf_op | source)
XLA Modules:
  0.0 807.7 jit_solution(13728828844367373214)
XLA Ops:
  16.6 89.1 %all-gather.12.cloned.1.call-done = f32[16384,256]{1,0:T(8,128)} async-done(((f32[2048,256]{1,0:T(8,128)}), f32[16384,256]{1,0:T(8,128)}) %all-gather.12.cloned.1.call-update) | async-done | bytes 16777232 | tf_op jit(solution)/shard_map/all_gather | solution.py:9
  105.7 8.5 %reduce_sum.36 = f32[2048,256]{1,0:T(8,128)} reduce(f32[8,2048,256]{2,1,0:T(8,128)} %bitcast.84, f32[]{:T(128)} %constant.65.clone.1), dimensions={0}, to_apply=%region_0.1 | reduce | flops 3670016 | bytes 18874372 | tf_op jit(solution)/shard_map/reduce_sum | solution.py:10
  114.3 83.1 %all-gather.14.cloned.1.call-done = f32[16384,256]{1,0:T(8,128)} async-done(((f32[2048,256]{1,0:T(8,128)}), f32[16384,256]{1,0:T(8,128)}) %all-gather.14.cloned.1.call-update) | async-done | bytes 16777232 | tf_op jit(solution)/shard_map/all_gather | solution.py:9
  197.4 8.5 %reduce_sum.37 = f32[2048,256]{1,0:T(8,128)} reduce(f32[8,2048,256]{2,1,0:T(8,128)} %bitcast.85, f32[]{:T(128)} %constant.65.clone.1), dimensions={0}, to_apply=%region_1.2 | reduce | flops 3670016 | bytes 18874372 | tf_op jit(solution)/shard_map/reduce_sum | solution.py:10
  210.3 126.4 %while.22 = (s32[]{:T(128)}, f32[16,32768]{1,0:T(8,128)S(1)}, s32[4,64]{1,0:T(4,128)S(1)}, f32[4,64,128,128]{3,2,1,0:T(8,128)}, s32[4,64]{1,0:T(4,128)S(1)}, /*i...) while((s32[]{:T(128)}, f32[16,32768]{1,0:T(8,128)S(1)}, ...), condition=%wide.region_3.5_spmd.clone, body=%wide.region_2.4_spmd.clone.sunk | while | flops 3629124096 | bytes 67116272 | solution.py:49
  216.8 11.7 %broadcast_multiply_fusion.4 = f32[64,128,256]{2,1,0:T(8,128)S(1)} fusion(f32[64]{0:T(128)S(1)} %fusion.59, f32[64,128,256]{2,1,0:T(8,128)} %gather_fusion, pred[64]{0:T(512)(128)(4,1)S(1)} %get-tuple-element.266, f32[4,64,128,128]{3,2,1,0:T(8,128)} %get-tuple-element.297, s32[]{:T(128)} %get-tuple-element.285), kind=kOutput, calls=%fused_computation.9.clone.1 | convolution fusion | flops 3225419776 | bytes 20972352 | tf_op jit(solution)/shard_map/while/body/eval_jaxpr/tij,tjf->tif/dot_general | solution.py:32
  228.6 8.0 copy.12
  242.0 6.5 gather_fusion
  248.5 11.7 %broadcast_multiply_fusion.4 = f32[64,128,256]{2,1,0:T(8,128)S(1)} fusion(f32[64]{0:T(128)S(1)} %fusion.59, f32[64,128,256]{2,1,0:T(8,128)} %gather_fusion, pred[64]{0:T(512)(128)(4,1)S(1)} %get-tuple-element.266, f32[4,64,128,128]{3,2,1,0:T(8,128)} %get-tuple-element.297, s32[]{:T(128)} %get-tuple-element.285), kind=kOutput, calls=%fused_computation.9.clone.1 | convolution fusion | flops 3225419776 | bytes 20972352 | tf_op jit(solution)/shard_map/while/body/eval_jaxpr/tij,tjf->tif/dot_general | solution.py:32
  260.2 8.0 copy.12
  273.6 6.5 gather_fusion
  280.1 11.7 %broadcast_multiply_fusion.4 = f32[64,128,256]{2,1,0:T(8,128)S(1)} fusion(f32[64]{0:T(128)S(1)} %fusion.59, f32[64,128,256]{2,1,0:T(8,128)} %gather_fusion, pred[64]{0:T(512)(128)(4,1)S(1)} %get-tuple-element.266, f32[4,64,128,128]{3,2,1,0:T(8,128)} %get-tuple-element.297, s32[]{:T(128)} %get-tuple-element.285), kind=kOutput, calls=%fused_computation.9.clone.1 | convolution fusion | flops 3225419776 | bytes 20972352 | tf_op jit(solution)/shard_map/while/body/eval_jaxpr/tij,tjf->tif/dot_general | solution.py:32
  291.8 8.0 copy.12
  311.7 11.7 %broadcast_multiply_fusion.4 = f32[64,128,256]{2,1,0:T(8,128)S(1)} fusion(f32[64]{0:T(128)S(1)} %fusion.59, f32[64,128,256]{2,1,0:T(8,128)} %gather_fusion, pred[64]{0:T(512)(128)(4,1)S(1)} %get-tuple-element.266, f32[4,64,128,128]{3,2,1,0:T(8,128)} %get-tuple-element.297, s32[]{:T(128)} %get-tuple-element.285), kind=kOutput, calls=%fused_computation.9.clone.1 | convolution fusion | flops 3225419776 | bytes 20972352 | tf_op jit(solution)/shard_map/while/body/eval_jaxpr/tij,tjf->tif/dot_general | solution.py:32
  323.4 8.0 copy.12
  338.6 43.5 %reduce-scatter.3.cloned.1.call-done = f32[512,256]{1,0:T(8,128)} async-done(((f32[2048,256]{1,0:T(8,128)}), f32[512,256]{1,0:T(8,128)}) %reduce-scatter.3.cloned.1.call-update) | async-done | bytes 524304 | tf_op jit(solution)/shard_map/reduce_scatter | solution.py:78
  384.6 45.0 %all-gather.10.cloned.1.call-done = f32[2048,256]{1,0:T(8,128)} async-done(((f32[512,256]{1,0:T(8,128)}), f32[2048,256]{1,0:T(8,128)}) %all-gather.10.cloned.1.call-update) | async-done | bytes 2097168 | tf_op jit(solution)/shard_map/all_gather | solution.py:83
  434.1 88.1 %all-gather.16.cloned.1.call-done = f32[16384,256]{1,0:T(8,128)} async-done(((f32[2048,256]{1,0:T(8,128)}), f32[16384,256]{1,0:T(8,128)}) %all-gather.16.cloned.1.call-update) | async-done | bytes 16777232 | tf_op jit(solution)/shard_map/all_gather | solution.py:9
  522.2 8.5 %reduce_sum.38 = f32[2048,256]{1,0:T(8,128)} reduce(f32[8,2048,256]{2,1,0:T(8,128)} %bitcast.86, f32[]{:T(128)} %constant.65.clone.1), dimensions={0}, to_apply=%region_5.7 | reduce | flops 3670016 | bytes 18874372 | tf_op jit(solution)/shard_map/reduce_sum | solution.py:10
  530.7 83.0 %all-gather.18.cloned.1.call-done = f32[16384,256]{1,0:T(8,128)} async-done(((f32[2048,256]{1,0:T(8,128)}), f32[16384,256]{1,0:T(8,128)}) %all-gather.18.cloned.1.call-update) | async-done | bytes 16777232 | tf_op jit(solution)/shard_map/all_gather | solution.py:9
  613.7 8.5 %reduce_sum.39 = f32[2048,256]{1,0:T(8,128)} reduce(f32[8,2048,256]{2,1,0:T(8,128)} %bitcast.87, f32[]{:T(128)} %constant.65.clone.1), dimensions={0}, to_apply=%region_6.8 | reduce | flops 3670016 | bytes 18874372 | tf_op jit(solution)/shard_map/reduce_sum | solution.py:10
  626.6 126.4 %while.23 = (s32[]{:T(128)}, f32[16,32768]{1,0:T(8,128)S(1)}, s32[4,64]{1,0:T(4,128)S(1)}, f32[4,64,128,128]{3,2,1,0:T(8,128)}, s32[4,64]{1,0:T(4,128)S(1)}, /*i...) while((s32[]{:T(128)}, f32[16,32768]{1,0:T(8,128)S(1)}, ...), condition=%wide.region_8.10_spmd.clone, body=%wide.region_7.9_spmd.clone.sunk | while | flops 3629124096 | bytes 67116272 | solution.py:49
  633.2 11.7 %broadcast_multiply_fusion.5 = f32[64,128,256]{2,1,0:T(8,128)S(1)} fusion(f32[64]{0:T(128)S(1)} %fusion.64, f32[64,128,256]{2,1,0:T(8,128)} %gather_fusion.1, pred[64]{0:T(512)(128)(4,1)S(1)} %get-tuple-element.275, f32[4,64,128,128]{3,2,1,0:T(8,128)} %get-tuple-element.324, s32[]{:T(128)} %get-tuple-element.312), kind=kOutput, calls=%fused_computation.30.clone.1 | convolution fusion | flops 3225419776 | bytes 20972352 | tf_op jit(solution)/shard_map/while/body/eval_jaxpr/tij,tjf->tif/dot_general | solution.py:32
  644.9 8.0 copy.13
  658.3 6.5 gather_fusion.1
  664.8 11.7 %broadcast_multiply_fusion.5 = f32[64,128,256]{2,1,0:T(8,128)S(1)} fusion(f32[64]{0:T(128)S(1)} %fusion.64, f32[64,128,256]{2,1,0:T(8,128)} %gather_fusion.1, pred[64]{0:T(512)(128)(4,1)S(1)} %get-tuple-element.275, f32[4,64,128,128]{3,2,1,0:T(8,128)} %get-tuple-element.324, s32[]{:T(128)} %get-tuple-element.312), kind=kOutput, calls=%fused_computation.30.clone.1 | convolution fusion | flops 3225419776 | bytes 20972352 | tf_op jit(solution)/shard_map/while/body/eval_jaxpr/tij,tjf->tif/dot_general | solution.py:32
  676.5 8.0 copy.13
  696.4 11.7 %broadcast_multiply_fusion.5 = f32[64,128,256]{2,1,0:T(8,128)S(1)} fusion(f32[64]{0:T(128)S(1)} %fusion.64, f32[64,128,256]{2,1,0:T(8,128)} %gather_fusion.1, pred[64]{0:T(512)(128)(4,1)S(1)} %get-tuple-element.275, f32[4,64,128,128]{3,2,1,0:T(8,128)} %get-tuple-element.324, s32[]{:T(128)} %get-tuple-element.312), kind=kOutput, calls=%fused_computation.30.clone.1 | convolution fusion | flops 3225419776 | bytes 20972352 | tf_op jit(solution)/shard_map/while/body/eval_jaxpr/tij,tjf->tif/dot_general | solution.py:32
  708.1 8.0 copy.13
  728.0 11.7 %broadcast_multiply_fusion.5 = f32[64,128,256]{2,1,0:T(8,128)S(1)} fusion(f32[64]{0:T(128)S(1)} %fusion.64, f32[64,128,256]{2,1,0:T(8,128)} %gather_fusion.1, pred[64]{0:T(512)(128)(4,1)S(1)} %get-tuple-element.275, f32[4,64,128,128]{3,2,1,0:T(8,128)} %get-tuple-element.324, s32[]{:T(128)} %get-tuple-element.312), kind=kOutput, calls=%fused_computation.30.clone.1 | convolution fusion | flops 3225419776 | bytes 20972352 | tf_op jit(solution)/shard_map/while/body/eval_jaxpr/tij,tjf->tif/dot_general | solution.py:32
  739.8 8.0 copy.13
  754.6 43.8 %reduce-scatter.5.cloned.1.call-done = f32[512,256]{1,0:T(8,128)} async-done(((f32[2048,256]{1,0:T(8,128)}), f32[512,256]{1,0:T(8,128)}) %reduce-scatter.5.cloned.1.call-update) | async-done | bytes 524304 | tf_op jit(solution)/shard_map/reduce_scatter | solution.py:78
  (87 shorter events, 105.2 us)
Async XLA Ops:
  6.5 0.7 copy-start
  6.5 99.2 %all-gather.12.cloned.1.call-start = ((), (), s32[]{:S(2)}) async-start(), calls=%async_computation.5 | async-start | bytes 18874368 | tf_op jit(solution)/shard_map/all_gather | solution.py:9
  9.1 5.4 copy-start.3
  9.1 6.1 copy-start.4
  13.1 184.2 %all-gather.14.cloned.1.call-start = ((), (), s32[]{:S(2)}) async-start(), calls=%async_computation.6 | async-start | bytes 18874368 | tf_op jit(solution)/shard_map/all_gather | solution.py:9
  13.9 368.2 %reduce-scatter.3.cloned.1.call-start = ((), (), s32[]{:S(2)}) async-start(), calls=%async_computation.2 | async-start | bytes 2621440 | tf_op jit(solution)/shard_map/reduce_scatter | solution.py:78
  336.8 45.3 %copy-start.2 = (f32[2,256,256]{2,1,0:T(8,128)S(1)}, f32[2,256,256]{2,1,0:T(8,128)}, u32[]{:S(2)}) copy-start(f32[2,256,256]{2,1,0:T(8,128)} %param.19) | copy-start | bytes 1572868
  338.3 91.2 %all-gather.10.cloned.1.call-start = ((), (), s32[]{:S(2)}) async-start(), calls=%async_computation.3 | async-start | bytes 2621440 | tf_op jit(solution)/shard_map/all_gather | solution.py:83
  384.5 137.7 %all-gather.16.cloned.1.call-start = ((), (), s32[]{:S(2)}) async-start(), calls=%async_computation.7 | async-start | bytes 18874368 | tf_op jit(solution)/shard_map/all_gather | solution.py:9
  433.5 180.2 %all-gather.18.cloned.1.call-start = ((), (), s32[]{:S(2)}) async-start(), calls=%async_computation.8 | async-start | bytes 18874368 | tf_op jit(solution)/shard_map/all_gather | solution.py:9
  434.1 364.3 %reduce-scatter.5.cloned.1.call-start = ((), (), s32[]{:S(2)}) async-start(), calls=%async_computation.4 | async-start | bytes 2621440 | tf_op jit(solution)/shard_map/reduce_scatter | solution.py:78
  753.1 47.8 %copy-start.1 = (s32[4,2]{0,1:T(2,128)S(1)}, s32[4,2]{0,1:T(2,128)}, u32[]{:S(2)}) copy-start(s32[4,2]{0,1:T(2,128)} %param.18) | copy-start | bytes 100
Sparse Core Ops, SparseCore 0:
  13.2 92.4 all-gather.11
  107.6 89.7 all-gather.13
  338.4 43.6 reduce-scatter.2
  384.7 44.8 all-gather.9
  433.6 88.5 all-gather.15
  523.9 89.7 all-gather.17
  754.7 43.6 reduce-scatter.4
